TPU v7x, 32 devices: a whole 2x2x4 slice. The times are simulated.
32 devices in a mesh: wide: 8 (over z, x), grp: 4 (over y, core).
Axes of the slice: x: 2, y: 2, z: 4, core: 2. Of those that a mesh axis runs over, the one named last changes fastest.
Arguments:
- query_rows: bfloat16 [4096, 1280], P(('wide', 'grp')), may hold values from -9 to 9, as said below
- key_rows: bfloat16 [4096, 1280], P(('wide', 'grp')), may hold values from -9 to 9, as said below
- value_rows: bfloat16 [4096, 1280], P(('wide', 'grp')), may hold values from -6 to 6
- block_image: int32 [32], replicated, may hold values from 0 to 6, never falling along the last dimension, each value on 1 to 8 neighbouring positions
Outputs:
- attended: bfloat16 [4096, 1280], P(('wide', 'grp'))
Inputs may be any that keep to these rules, and one draw needn't show every extreme that they name: `query_rows`: Queries: entries bounded as stated. `key_rows`: Keys: entries bounded as stated. `block_image`: image numbers never fall along the window; every image covers 1 to 8 whole blocks and one covers exactly 8.
All inputs are finite; a program needn't handle non-finite values.
Results may differ from a plain program's by a relative error of at most 0.004.
Values may be sent and summed in bfloat16 or wider, within the bound.
A program may use at most 64 MiB of HBM per device.

v0:
```python
import math
import jax
import jax.numpy as jnp
from jax import lax
from jax.sharding import PartitionSpec as P

HDIM = 80
BLK = 128
MOST = 8
neg_large = -1e30


def from_behind(value, axis, steps):
    count = lax.axis_size(axis)
    leading, last = (max(0, -steps), min(count, count - steps))
    return lax.ppermute(value, axis, [(source, source + steps) for source in range(leading, last)])


def block_tokens(block_ids, block_rows):
    return jnp.broadcast_to(block_ids[:, None], (block_ids.shape[0], block_rows)).reshape(-1)


def fold_tile(totals, query_ids, query_head, key_head, value_head, key_ids, scale_value):
    live_pairs = query_ids[:, None] == key_ids[None, :]
    acc_out, run_max, run_den = totals
    scores = (
        jnp.einsum("qhd,khd->qhk", query_head, key_head, preferred_element_type=jnp.float32)
        * scale_value
    )
    scores = jnp.where(live_pairs[:, None, :], scores, neg_large)
    new_max = jnp.maximum(run_max, jnp.max(scores, axis=-1))
    weights = jnp.where(live_pairs[:, None, :], jnp.exp(scores - new_max[..., None]), 0.0)
    fading = jnp.exp(run_max - new_max)
    run_den = run_den * fading + jnp.sum(weights, axis=-1)
    acc_out = acc_out * fading[..., None] + jnp.einsum(
        "qhk,khd->qhd", weights.astype(jnp.bfloat16), value_head, preferred_element_type=jnp.float32
    )
    return (acc_out, new_max, run_den)


def fold_keys(totals, query_ids, query_head, key_head, value_head, key_ids, scale_value):
    current = tuple((member for member in totals))
    current = fold_tile(current, query_ids, query_head, key_head, value_head, key_ids, scale_value)
    return current


def body(query_rows, key_rows, value_rows, block_image):
    stacked = jnp.stack((query_rows, key_rows, value_rows))
    regrouped = lax.all_to_all(stacked, "grp", split_axis=2, concat_axis=1, tiled=True)
    local_rows = regrouped.shape[1]
    head_count = regrouped.shape[2] // HDIM
    shaped = regrouped.reshape(3, local_rows, head_count, HDIM)
    query_head = shaped[0]
    key_value = shaped[1:]
    blocks_here = local_rows // BLK
    wide_count = lax.axis_size("wide")
    position = lax.axis_index("wide")
    scale_value = 1.0 / math.sqrt(HDIM)
    query_ids = block_tokens(
        lax.dynamic_slice_in_dim(block_image, position * blocks_here, blocks_here), BLK
    )

    def source_ids(source):
        inside = (source >= 0) & (source < wide_count)
        clipped = jnp.clip(source, 0, wide_count - 1)
        found_ids = block_tokens(
            lax.dynamic_slice_in_dim(block_image, clipped * blocks_here, blocks_here), BLK
        )
        return jnp.where(inside, found_ids, -2)

    totals = (
        jnp.zeros((local_rows, head_count, HDIM), jnp.float32),
        jnp.full((local_rows, head_count), neg_large, jnp.float32),
        jnp.zeros((local_rows, head_count), jnp.float32),
    )
    reach_steps = min(wide_count - 1, (MOST + blocks_here - 2) // blocks_here)
    totals = fold_keys(
        totals, query_ids, query_head, key_value[0], key_value[1], query_ids, scale_value
    )
    for distance in range(1, reach_steps + 1):
        arrived = from_behind(key_value, "wide", distance)
        totals = fold_keys(
            totals,
            query_ids,
            query_head,
            arrived[0],
            arrived[1],
            source_ids(position - distance),
            scale_value,
        )
        arrived = from_behind(key_value, "wide", -distance)
        totals = fold_keys(
            totals,
            query_ids,
            query_head,
            arrived[0],
            arrived[1],
            source_ids(position + distance),
            scale_value,
        )
    acc_out, run_max, run_den = totals
    result = (
        (acc_out / run_den[..., None]).astype(jnp.bfloat16).reshape(local_rows, head_count * HDIM)
    )
    restored = lax.all_to_all(result, "grp", split_axis=0, concat_axis=1, tiled=True)
    return restored


def solution(mesh):
    return jax.shard_map(
        body,
        mesh=mesh,
        in_specs=(
            P(("wide", "grp"), None),
            P(("wide", "grp"), None),
            P(("wide", "grp"), None),
            P(),
        ),
        out_specs=P(("wide", "grp"), None),
        check_vma=False,
    )
```

profile of v0, /device:TPU:24, one launch (start us, length us, event | category | flops | bytes accessed | tf_op | source)
XLA Modules:
  0.0 93.7 jit_solution(12908256977121639371)
XLA Ops:
  0.0 0.0 copy-start
  0.0 1.3 %pad_maximum_fusion = bf16[3,128,1280]{2,1,0:T(8,128)(2,1)S(1)} fusion(bf16[1,128,1280]{2,1,0:T(8,128)(2,1)} %bitcast.190, bf16[1,128,1280]{2,1,0:T(8,128)(2,1)} %bitcast.191, bf16[1,128,1280]{2,1,0:T(8,128)(2,1)} %bitcast.192), kind=kLoop, calls=%fused_computation.51 | loop fusion | flops 983040 | bytes 1966080 | tf_op jit(solution)/shard_map/stack | solution.py:48
  1.3 2.2 %copy.41 = bf16[3,128,1280]{1,0,2:T(4,128)(2,1)} copy(bf16[3,128,1280]{2,1,0:T(8,128)(2,1)S(1)} %pad_maximum_fusion) | data formatting | bytes 1966080 | tf_op jit(solution)/shard_map/stack | solution.py:48
  3.5 3.5 %all-to-all-start = ((bf16[3,128,1280]{1,0,2:T(4,128)(2,1)}), bf16[3,128,1280]{1,0,2:T(4,128)(2,1)S(1)}, u32[]{:S(2)}, u32[]{:S(2)}) async-start(bf16[3,128,1280]{1,0,2:T(4,128)(2,1)} %copy.41), calls=%async_computation | async-start | bytes 2621440 | tf_op jit(solution)/shard_map/all_to_all | solution.py:49
  7.0 0.0 copy-done
  7.1 0.1 broadcast_select_fusion.3
  7.1 0.1 broadcast_bitcast_fusion.4
  7.2 0.1 broadcast_bitcast_fusion.2
  7.3 0.1 broadcast_bitcast_fusion
  7.4 16.9 %all-to-all-done = bf16[3,128,1280]{1,0,2:T(4,128)(2,1)S(1)} async-done(((bf16[3,128,1280]{1,0,2:T(4,128)(2,1)}), bf16[3,128,1280]{1,0,2:T(4,128)(2,1)S(1)}, u32[]{:S(2)}, u32[]{:S(2)}) %all-to-all-start) | async-done | bytes 983072 | tf_op jit(solution)/shard_map/all_to_all | solution.py:49
  24.2 0.1 copy.42
  24.4 0.5 copy.47
  24.9 1.1 %slice.48 = bf16[2,512,4,80]{1,3,2,0:T(8,128)(2,1)} reshape(bf16[2,4,128,320]{2,1,3,0:T(4,128)(2,1)S(1)} %copy.47) | data formatting | bytes 1310720 | tf_op jit(solution)/shard_map/slice | solution.py:54
  26.0 3.3 %collective-permute-start.1 = (bf16[2,512,4,80]{1,3,2,0:T(8,128)(2,1)}, bf16[2,512,4,80]{1,3,2,0:T(8,128)(2,1)}, u32[]{:S(2)}, u32[]{:S(2)}) collective-permute-start(bf16[2,512,4,80]{1,3,2,0:T(8,128)(2,1)} %slice.48), channel_id=1, source_target_pairs={{4,0},{8,4},{12,8},{16,12},{20,16},{24,20},{28,24},{5,1},{9,5},{13... | collective-permute-start | bytes 1966088 | tf_op jit(solution)/shard_map/ppermute | solution.py:16
  29.3 0.9 broadcast_compare_fusion.4
  30.2 3.2 %collective-permute-start.3 = (bf16[2,512,4,80]{1,3,2,0:T(8,128)(2,1)}, bf16[2,512,4,80]{1,3,2,0:T(8,128)(2,1)}, u32[]{:S(2)}, u32[]{:S(2)}) collective-permute-start(bf16[2,512,4,80]{1,3,2,0:T(8,128)(2,1)} %slice.48), channel_id=1, source_target_pairs={{8,0},{12,4},{16,8},{20,12},{24,16},{28,20},{9,1},{13,5},{17,9},{2... | collective-permute-start | bytes 1966088 | tf_op jit(solution)/shard_map/ppermute | solution.py:16
  33.4 1.3 %collective-permute-start.2 = (bf16[2,512,4,80]{1,3,2,0:T(8,128)(2,1)}, bf16[2,512,4,80]{1,3,2,0:T(8,128)(2,1)}, u32[]{:S(2)}, u32[]{:S(2)}) collective-permute-start(bf16[2,512,4,80]{1,3,2,0:T(8,128)(2,1)} %slice.48), channel_id=1, source_target_pairs={{0,8},{4,12},{8,16},{12,20},{16,24},{20,28},{1,9},{5,13},{9,17},{1... | collective-permute-start | bytes 1966088 | tf_op jit(solution)/shard_map/ppermute | solution.py:16
  34.7 2.7 %collective-permute-start = (bf16[2,512,4,80]{1,3,2,0:T(8,128)(2,1)}, bf16[2,512,4,80]{1,3,2,0:T(8,128)(2,1)}, u32[]{:S(2)}, u32[]{:S(2)}) collective-permute-start(bf16[2,512,4,80]{1,3,2,0:T(8,128)(2,1)} %slice.48), channel_id=1, source_target_pairs={{0,4},{4,8},{8,12},{12,16},{16,20},{20,24},{24,28},{1,5},{5,9},{9,... | collective-permute-start | bytes 1966088 | tf_op jit(solution)/shard_map/ppermute | solution.py:16
  37.5 0.1 fusion.100
  37.5 0.3 copy.45
  37.8 0.1 squeeze.35
  37.9 0.3 copy.44
  38.2 0.1 squeeze.34
  38.3 0.3 copy.43
  38.6 0.1 squeeze.33
  38.7 1.0 %fusion = (f32[512,4]{0,1:T(4,128)S(1)}, f32[4,512,512]{2,1,0:T(8,128)S(1)}) fusion(pred[512,512]{0,1:T(8,128)(4,1)S(1)} %get-tuple-element.19, bf16[512,4,80]{0,2,1:T(8,128)(2,1)S(1)} %squeeze.33, bf16[512,4,80]{0,2,1:T(8,128)(2,1)S(1)} %squeeze.34), kind=kOutput, calls=%fused_computation.10 | convolution fusion | flops 170915840 | bytes 5120000 | tf_op jit(solution)/shard_map/qhd,khd->qhk/dot_general | solution.py:27
  39.7 5.1 %collective-permute-done.1 = bf16[2,512,4,80]{1,3,2,0:T(8,128)(2,1)} collective-permute-done((bf16[2,512,4,80]{1,3,2,0:T(8,128)(2,1)}, bf16[2,512,4,80]{1,3,2,0:T(8,128)(2,1)}, u32[]{:S(2)}, u32[]{:S(2)}) %collective-permute-start.1) | collective-permute-done | bytes 655392 | tf_op jit(solution)/shard_map/ppermute | solution.py:16
  44.8 1.9 %fusion.2 = (f32[512,4]{0,1:T(4,128)S(1)}, f32[4,512,512]{2,1,0:T(8,128)S(1)}) fusion(pred[512,512]{0,1:T(8,128)(4,1)S(1)} %get-tuple-element.20, bf16[512,4,80]{0,2,1:T(8,128)(2,1)S(1)} %squeeze.34, bf16[2,512,4,80]{1,3,2,0:T(8,128)(2,1)} %collective-permute-done.1), kind=kOutput, calls=%fused_computation.12 | convolution fusion | flops 170915840 | bytes 5120000 | tf_op jit(solution)/shard_map/qhd,khd->qhk/dot_general | solution.py:27
  46.7 4.5 %collective-permute-done.2 = bf16[2,512,4,80]{1,3,2,0:T(8,128)(2,1)} collective-permute-done((bf16[2,512,4,80]{1,3,2,0:T(8,128)(2,1)}, bf16[2,512,4,80]{1,3,2,0:T(8,128)(2,1)}, u32[]{:S(2)}, u32[]{:S(2)}) %collective-permute-start.2) | collective-permute-done | bytes 655392 | tf_op jit(solution)/shard_map/ppermute | solution.py:16
  51.2 1.9 %fusion.3 = (f32[512,4]{0,1:T(4,128)S(1)}, f32[4,512,512]{2,1,0:T(8,128)S(1)}) fusion(pred[512,512]{0,1:T(8,128)(4,1)S(1)} %get-tuple-element.21, bf16[512,4,80]{0,2,1:T(8,128)(2,1)S(1)} %squeeze.34, bf16[2,512,4,80]{1,3,2,0:T(8,128)(2,1)} %collective-permute-done.2), kind=kOutput, calls=%fused_computation.13 | convolution fusion | flops 170915840 | bytes 5120000 | tf_op jit(solution)/shard_map/qhd,khd->qhk/dot_general | solution.py:27
  53.2 4.2 %collective-permute-done.3 = bf16[2,512,4,80]{1,3,2,0:T(8,128)(2,1)} collective-permute-done((bf16[2,512,4,80]{1,3,2,0:T(8,128)(2,1)}, bf16[2,512,4,80]{1,3,2,0:T(8,128)(2,1)}, u32[]{:S(2)}, u32[]{:S(2)}) %collective-permute-start.3) | collective-permute-done | bytes 655392 | tf_op jit(solution)/shard_map/ppermute | solution.py:16
  57.4 1.9 %fusion.4 = (f32[512,4]{0,1:T(4,128)S(1)}, f32[4,512,512]{2,1,0:T(8,128)S(1)}) fusion(pred[512,512]{0,1:T(8,128)(4,1)S(1)} %get-tuple-element.22, bf16[512,4,80]{0,2,1:T(8,128)(2,1)S(1)} %squeeze.34, bf16[2,512,4,80]{1,3,2,0:T(8,128)(2,1)} %collective-permute-done.3), kind=kOutput, calls=%fused_computation.14 | convolution fusion | flops 170915840 | bytes 5120000 | tf_op jit(solution)/shard_map/qhd,khd->qhk/dot_general | solution.py:27
  59.4 6.0 %collective-permute-done = bf16[2,512,4,80]{1,3,2,0:T(8,128)(2,1)} collective-permute-done((bf16[2,512,4,80]{1,3,2,0:T(8,128)(2,1)}, bf16[2,512,4,80]{1,3,2,0:T(8,128)(2,1)}, u32[]{:S(2)}, u32[]{:S(2)}) %collective-permute-start) | collective-permute-done | bytes 655392 | tf_op jit(solution)/shard_map/ppermute | solution.py:16
  65.4 1.9 %fusion.1 = (f32[512,4]{0,1:T(4,128)S(1)}, f32[4,512,512]{2,1,0:T(8,128)S(1)}) fusion(pred[512,512]{0,1:T(8,128)(4,1)S(1)} %get-tuple-element.23, bf16[512,4,80]{0,2,1:T(8,128)(2,1)S(1)} %squeeze.34, bf16[2,512,4,80]{1,3,2,0:T(8,128)(2,1)} %collective-permute-done), kind=kOutput, calls=%fused_computation.11 | convolution fusion | flops 170915840 | bytes 5120000 | tf_op jit(solution)/shard_map/qhd,khd->qhk/dot_general | solution.py:27
  67.4 1.0 %fusion.13 = f32[512,4]{0,1:T(4,128)S(1)} fusion(f32[4,512,512]{2,1,0:T(8,128)S(1)} %get-tuple-element.30, f32[512,4]{0,1:T(4,128)S(1)} %get-tuple-element.10, pred[512,512]{0,1:T(8,128)(4,1)S(1)} %get-tuple-element.22), kind=kLoop, calls=%fused_computation.23 | loop fusion | flops 5240832 | bytes 4472832 | tf_op jit(solution)/shard_map/reduce_sum | solution.py:34
  68.4 1.1 %fusion.11 = f32[512,4]{0,1:T(4,128)S(1)} fusion(f32[4,512,512]{2,1,0:T(8,128)S(1)} %get-tuple-element.32, f32[512,4]{0,1:T(4,128)S(1)} %get-tuple-element.11, pred[512,512]{0,1:T(8,128)(4,1)S(1)} %get-tuple-element.21), kind=kLoop, calls=%fused_computation.21 | loop fusion | flops 5240832 | bytes 4472832 | tf_op jit(solution)/shard_map/reduce_sum | solution.py:34
  69.5 1.0 %fusion.9 = f32[512,4]{0,1:T(4,128)S(1)} fusion(f32[4,512,512]{2,1,0:T(8,128)S(1)} %get-tuple-element.34, f32[512,4]{0,1:T(4,128)S(1)} %get-tuple-element.12, pred[512,512]{0,1:T(8,128)(4,1)S(1)} %get-tuple-element.20), kind=kLoop, calls=%fused_computation.19 | loop fusion | flops 5240832 | bytes 4472832 | tf_op jit(solution)/shard_map/reduce_sum | solution.py:34
  70.5 1.1 %fusion.5 = f32[512,4]{0,1:T(4,128)S(1)} fusion(f32[4,512,512]{2,1,0:T(8,128)S(1)} %get-tuple-element.38, f32[512,4]{0,1:T(4,128)S(1)} %get-tuple-element.18, pred[512,512]{0,1:T(8,128)(4,1)S(1)} %get-tuple-element.19), kind=kLoop, calls=%fused_computation.15 | loop fusion | flops 5240832 | bytes 4472832 | tf_op jit(solution)/shard_map/reduce_sum | solution.py:34
  71.6 1.1 %fusion.7 = f32[512,4]{0,1:T(4,128)S(1)} fusion(f32[4,512,512]{2,1,0:T(8,128)S(1)} %get-tuple-element.36, f32[512,4]{0,1:T(4,128)S(1)} %get-tuple-element.13, pred[512,512]{0,1:T(8,128)(4,1)S(1)} %get-tuple-element.23), kind=kLoop, calls=%fused_computation.17 | loop fusion | flops 5240832 | bytes 4472832 | tf_op jit(solution)/shard_map/reduce_sum | solution.py:34
  72.7 1.5 %fusion.69 = f32[512,4,80]{0,2,1:T(8,128)S(1)} fusion(bf16[512,4,80]{0,2,1:T(8,128)(2,1)S(1)} %squeeze.35, f32[4,512,512]{2,1,0:T(8,128)S(1)} %get-tuple-element.38, f32[512,4]{0,1:T(4,128)S(1)} %get-tuple-element.18, pred[512,512]{0,1:T(8,128)(4,1)S(1)} %get-tuple-element.19, f32[512,4]{0,1:T(4,128)S(1)} %get-tuple-element.9, ...), kind=kOutput, calls=%fused_computation.48 | convolution fusion | flops 173342720 | bytes 5464064 | tf_op jit(solution)/shard_map/qhk,khd->qhd/dot_general | solution.py:35
  74.2 2.3 %fusion.42 = f32[512,4,80]{0,2,1:T(8,128)S(1)} fusion(f32[4,512,512]{2,1,0:T(8,128)S(1)} %get-tuple-element.30, f32[512,4]{0,1:T(4,128)S(1)} %get-tuple-element.10, pred[512,512]{0,1:T(8,128)(4,1)S(1)} %get-tuple-element.22, bf16[2,512,4,80]{1,3,2,0:T(8,128)(2,1)} %collective-permute-done.3), kind=kOutput, calls=%fused_computation.39 | convolution fusion | flops 173015040 | bytes 5447680 | tf_op jit(solution)/shard_map/qhk,khd->qhd/dot_general | solution.py:35
  76.5 2.3 %fusion.39 = f32[512,4,80]{0,2,1:T(8,128)S(1)} fusion(f32[4,512,512]{2,1,0:T(8,128)S(1)} %get-tuple-element.32, f32[512,4]{0,1:T(4,128)S(1)} %get-tuple-element.11, pred[512,512]{0,1:T(8,128)(4,1)S(1)} %get-tuple-element.21, bf16[2,512,4,80]{1,3,2,0:T(8,128)(2,1)} %collective-permute-done.2), kind=kOutput, calls=%fused_computation.38 | convolution fusion | flops 173015040 | bytes 5447680 | tf_op jit(solution)/shard_map/qhk,khd->qhd/dot_general | solution.py:35
  78.8 2.3 %fusion.36 = f32[512,4,80]{0,2,1:T(8,128)S(1)} fusion(f32[4,512,512]{2,1,0:T(8,128)S(1)} %get-tuple-element.34, f32[512,4]{0,1:T(4,128)S(1)} %get-tuple-element.12, pred[512,512]{0,1:T(8,128)(4,1)S(1)} %get-tuple-element.20, bf16[2,512,4,80]{1,3,2,0:T(8,128)(2,1)} %collective-permute-done.1), kind=kOutput, calls=%fused_computation.37 | convolution fusion | flops 173015040 | bytes 5447680 | tf_op jit(solution)/shard_map/qhk,khd->qhd/dot_general | solution.py:35
  81.1 2.4 %fusion.75 = bf16[512,4,80]{0,2,1:T(8,128)(2,1)S(1)} fusion(f32[512,4,80]{0,2,1:T(8,128)S(1)} %fusion.42, f32[512,4,80]{0,2,1:T(8,128)S(1)} %fusion.39, f32[512,4,80]{0,2,1:T(8,128)S(1)} %fusion.36, f32[512,4,80]{0,2,1:T(8,128)S(1)} %fusion.69, f32[4,512,512]{2,1,0:T(8,128)S(1)} %get-tuple-element.36, f32[512,4]{0,1:T(4,128)S(1)} %get-tuple-element.13, ...), kind=kOutput, calls=%fused_computation.50 | convolution fusion | flops 174489600 | bytes 7774208 | tf_op jit(solution)/shard_map/qhk,khd->qhd/dot_general | solution.py:35
  83.5 0.1 all_to_all.28
  83.7 9.1 %all_to_all.34 = bf16[4,128,320]{1,2,0:T(8,128)(2,1)S(1)} all-to-all(bf16[4,128,320]{1,2,0:T(8,128)(2,1)S(1)} %copy.52), channel_id=1, replica_groups=mesh['wide'=8,'grp'=4] {'grp'}, dimensions={0} | all-to-all | bytes 655360 | tf_op jit(solution)/shard_map/all_to_all | solution.py:105
  92.8 0.9 copy.53
  (4 shorter events, 0.1 us)
Async XLA Ops:
  0.0 7.0 %copy-start = (s32[32]{0:T(128)S(1)}, s32[32]{0:T(128)}, u32[]{:S(2)}) copy-start(s32[32]{0:T(128)} %param.7) | copy-start | bytes 388
  3.5 20.8 %all-to-all-start = ((bf16[3,128,1280]{1,0,2:T(4,128)(2,1)}), bf16[3,128,1280]{1,0,2:T(4,128)(2,1)S(1)}, u32[]{:S(2)}, u32[]{:S(2)}) async-start(bf16[3,128,1280]{1,0,2:T(4,128)(2,1)} %copy.41), calls=%async_computation | async-start | bytes 2621440 | tf_op jit(solution)/shard_map/all_to_all | solution.py:49
  26.0 18.7 %collective-permute-start.1 = (bf16[2,512,4,80]{1,3,2,0:T(8,128)(2,1)}, bf16[2,512,4,80]{1,3,2,0:T(8,128)(2,1)}, u32[]{:S(2)}, u32[]{:S(2)}) collective-permute-start(bf16[2,512,4,80]{1,3,2,0:T(8,128)(2,1)} %slice.48), channel_id=1, source_target_pairs={{4,0},{8,4},{12,8},{16,12},{20,16},{24,20},{28,24},{5,1},{9,5},{13... | collective-permute-start | bytes 1966088 | tf_op jit(solution)/shard_map/ppermute | solution.py:16
  30.2 27.2 %collective-permute-start.3 = (bf16[2,512,4,80]{1,3,2,0:T(8,128)(2,1)}, bf16[2,512,4,80]{1,3,2,0:T(8,128)(2,1)}, u32[]{:S(2)}, u32[]{:S(2)}) collective-permute-start(bf16[2,512,4,80]{1,3,2,0:T(8,128)(2,1)} %slice.48), channel_id=1, source_target_pairs={{8,0},{12,4},{16,8},{20,12},{24,16},{28,20},{9,1},{13,5},{17,9},{2... | collective-permute-start | bytes 1966088 | tf_op jit(solution)/shard_map/ppermute | solution.py:16
  33.4 17.8 %collective-permute-start.2 = (bf16[2,512,4,80]{1,3,2,0:T(8,128)(2,1)}, bf16[2,512,4,80]{1,3,2,0:T(8,128)(2,1)}, u32[]{:S(2)}, u32[]{:S(2)}) collective-permute-start(bf16[2,512,4,80]{1,3,2,0:T(8,128)(2,1)} %slice.48), channel_id=1, source_target_pairs={{0,8},{4,12},{8,16},{12,20},{16,24},{20,28},{1,9},{5,13},{9,17},{1... | collective-permute-start | bytes 1966088 | tf_op jit(solution)/shard_map/ppermute | solution.py:16
  34.7 30.7 %collective-permute-start = (bf16[2,512,4,80]{1,3,2,0:T(8,128)(2,1)}, bf16[2,512,4,80]{1,3,2,0:T(8,128)(2,1)}, u32[]{:S(2)}, u32[]{:S(2)}) collective-permute-start(bf16[2,512,4,80]{1,3,2,0:T(8,128)(2,1)} %slice.48), channel_id=1, source_target_pairs={{0,4},{4,8},{8,12},{12,16},{16,20},{20,24},{24,28},{1,5},{5,9},{9,... | collective-permute-start | bytes 1966088 | tf_op jit(solution)/shard_map/ppermute | solution.py:16
where the time goes:
time: 94.3 us; the launch traced here: 93.7 us
  waiting for transfers between devices  36.7 us (39%)
  matrix products  19.6 us (21%)
  starting transfers between devices  14 us (15%)
  blocking collectives  9.08 us (10%)
  other arithmetic  7.57 us (8%)
  local copies, waits for them, and re-layouts  6.44 us (7%)
    ppermute x4, waiting for transfers between devices, from_behind(): lax.ppermute(value, axis, [(source, source + steps) for source in range(l...  19.9 us
    all_to_all x1, waiting for transfers between devices, body(): lax.all_to_all(stacked, 'grp', split_axis=2, concat_axis=1, tiled=True)  16.9 us
    dot_general x5, matrix products, fold_tile(): jnp.einsum('qhk,khd->qhd', weights.astype(jnp.bfloat16), value_head, pref...  10.9 us
    ppermute x4, starting transfers between devices, from_behind(): lax.ppermute(value, axis, [(source, source + steps) for source in range(l...  10.5 us
    all_to_all x1, blocking collectives, body(): lax.all_to_all(result, 'grp', split_axis=0, concat_axis=1, tiled=True)  9.08 us
    dot_general x5, matrix products, fold_tile(): jnp.einsum('qhd,khd->qhk', query_head, key_head, preferred_element_type=j...  8.72 us
    reduce_sum x5, other arithmetic, fold_tile(): run_den = run_den * fading + jnp.sum(weights, axis=-1)  5.27 us
    all_to_all x1, starting transfers between devices, body(): lax.all_to_all(stacked, 'grp', split_axis=2, concat_axis=1, tiled=True)  3.54 us
  transfers between devices with their start and end apart: 5, of which 5 were waited for; matrix products, arithmetic and copies ran while one was open for 10% of the time, Pallas kernels for 0%

commit v1 on v0

--- a/solution.py
+++ b/solution.py
@@ -8,6 +8,18 @@
 BLK = 128
 MOST = 8
 neg_large = -1e30
+
+
+def launch_notes(original, join_dim, array_dim):
+    return jnp.concatenate(
+        lax.all_to_all(
+            jnp.stack(jnp.split(original, lax.axis_size("grp"), axis=join_dim), axis=0),
+            axis_name="grp",
+            split_axis=0,
+            concat_axis=0,
+        ),
+        axis=array_dim,
+    )
 
 
 def from_behind(value, axis, steps):
@@ -46,7 +58,7 @@
 
 def body(query_rows, key_rows, value_rows, block_image):
     stacked = jnp.stack((query_rows, key_rows, value_rows))
-    regrouped = lax.all_to_all(stacked, "grp", split_axis=2, concat_axis=1, tiled=True)
+    regrouped = launch_notes(stacked, 2, 1)
     local_rows = regrouped.shape[1]
     head_count = regrouped.shape[2] // HDIM
     shaped = regrouped.reshape(3, local_rows, head_count, HDIM)

time: 94.3 us -> 92 us (0.976)
  waiting for transfers between devices: 36.7 us -> 33.2 us
  local copies, waits for them, and re-layouts: 6.44 us -> 7.74 us
    unnamed x2 -> x5, local copies, waits for them, and re-layouts: 0.01 us -> 3.56 us
    all_to_all x1, waiting for transfers between devices: 16.9 us -> 13.4 us  [launch_notes(): lax.all_to_all(jnp.stack(jnp.split(original, lax.axis_size('grp'), axis=j...]
    another operation x1, local copies, waits for them, and re-layouts: 2.18 us -> 0.07 us  [launch_notes(): jnp.stack(jnp.split(original, lax.axis_size('grp'), axis=join_dim), axis=0)]
    another operation x1, other arithmetic: 1.29 us -> 0.11 us  [body(): stacked = jnp.stack((query_rows, key_rows, value_rows))]
    another operation x0 -> x1, other arithmetic: none -> 1.08 us  [launch_notes(): jnp.stack(jnp.split(original, lax.axis_size('grp'), axis=join_dim), axis=0)]
where the time goes in v1:
time: 92 us; the launch traced here: 91.3 us
  waiting for transfers between devices  33.2 us (36%)
  matrix products  19.6 us (21%)
  starting transfers between devices  14 us (15%)
  blocking collectives  9.08 us (10%)
  local copies, waits for them, and re-layouts  7.74 us (8%)
  other arithmetic  7.47 us (8%)
    ppermute x4, waiting for transfers between devices, from_behind(): lax.ppermute(value, axis, [(source, source + steps) for source in range(l...  19.9 us
    all_to_all x1, waiting for transfers between devices, launch_notes(): lax.all_to_all(jnp.stack(jnp.split(original, lax.axis_size('grp'), axis=j...  13.4 us
    dot_general x5, matrix products, fold_tile(): jnp.einsum('qhk,khd->qhd', weights.astype(jnp.bfloat16), value_head, pref...  10.9 us
    ppermute x4, starting transfers between devices, from_behind(): lax.ppermute(value, axis, [(source, source + steps) for source in range(l...  10.5 us
    all_to_all x1, blocking collectives, body(): lax.all_to_all(result, 'grp', split_axis=0, concat_axis=1, tiled=True)  9.08 us
    dot_general x5, matrix products, fold_tile(): jnp.einsum('qhd,khd->qhk', query_head, key_head, preferred_element_type=j...  8.73 us
    reduce_sum x5, other arithmetic, fold_tile(): run_den = run_den * fading + jnp.sum(weights, axis=-1)  5.27 us
    unnamed x5, local copies, waits for them, and re-layouts  3.56 us
  transfers between devices with their start and end apart: 5, of which 5 were waited for; matrix products, arithmetic and copies ran while one was open for 10% of the time, Pallas kernels for 0%

profile of v1, /device:TPU:24, one launch (start us, length us, event | category | flops | bytes accessed | tf_op | source)
XLA Modules:
  0.0 91.3 jit_solution(7949446375103990647)
XLA Ops:
  0.0 1.2 %copy.26 = bf16[128,1280]{0,1:T(8,128)(2,1)S(1)} copy(bf16[128,1280]{1,0:T(8,128)(2,1)} %param.4) | data formatting | bytes 655360 | tf_op args[0]
  1.2 1.2 %copy.27 = bf16[128,1280]{0,1:T(8,128)(2,1)S(1)} copy(bf16[128,1280]{1,0:T(8,128)(2,1)} %param.5) | data formatting | bytes 655360 | tf_op args[1]
  2.4 0.0 copy-start
  2.4 1.2 %copy.28 = bf16[128,1280]{0,1:T(8,128)(2,1)S(1)} copy(bf16[128,1280]{1,0:T(8,128)(2,1)} %param.6) | data formatting | bytes 655360 | tf_op args[2]
  3.6 0.1 pad_maximum_fusion
  3.7 0.1 slice_bitcast_fusion.19
  3.8 1.1 %pad_maximum_fusion.1 = bf16[4,3,128,320]{2,3,1,0:T(8,128)(2,1)} fusion(bf16[1,3,128,320]{2,3,1,0:T(8,128)(2,1)S(1)} %get-tuple-element.18, bf16[1,3,128,320]{2,3,1,0:T(8,128)(2,1)S(1)} %get-tuple-element.19, bf16[1,3,128,320]{2,3,1,0:T(8,128)(2,1)S(1)} %get-tuple-element.20, bf16[1,3,128,320]{2,3,1,0:T(8,128)(2,1)S(1)} %get-tuple-element.17), kind=kLoop, calls=%fused_computation.52 | loop fusion | flops 1474560 | bytes 1966080 | tf_op jit(solution)/shard_map/stack | solution.py:16
  4.8 3.5 %all-to-all-start = ((bf16[4,3,128,320]{2,3,1,0:T(8,128)(2,1)}), bf16[4,3,128,320]{2,3,1,0:T(8,128)(2,1)S(1)}, u32[]{:S(2)}, u32[]{:S(2)}) async-start(bf16[4,3,128,320]{2,3,1,0:T(8,128)(2,1)} %pad_maximum_fusion.1), calls=%async_computation | async-start | bytes 1966080 | tf_op jit(solution)/shard_map/all_to_all | solution.py:15
  8.4 0.0 copy-done
  8.4 0.1 broadcast_select_fusion.3
  8.5 0.1 broadcast_bitcast_fusion.4
  8.6 0.1 broadcast_bitcast_fusion.2
  8.6 0.1 broadcast_bitcast_fusion
  8.7 13.4 %all-to-all-done = bf16[4,3,128,320]{2,3,1,0:T(8,128)(2,1)S(1)} async-done(((bf16[4,3,128,320]{2,3,1,0:T(8,128)(2,1)}), bf16[4,3,128,320]{2,3,1,0:T(8,128)(2,1)S(1)}, u32[]{:S(2)}, u32[]{:S(2)}) %all-to-all-start) | async-done | bytes 983072 | tf_op jit(solution)/shard_map/all_to_all | solution.py:15
  22.1 0.5 copy.33
  22.6 1.1 %slice.48 = bf16[2,512,4,80]{1,3,2,0:T(8,128)(2,1)} reshape(bf16[2,4,128,320]{2,1,3,0:T(4,128)(2,1)S(1)} %copy.33) | data formatting | bytes 1310720 | tf_op jit(solution)/shard_map/slice | solution.py:66
  23.7 3.3 %collective-permute-start.1 = (bf16[2,512,4,80]{1,3,2,0:T(8,128)(2,1)}, bf16[2,512,4,80]{1,3,2,0:T(8,128)(2,1)}, u32[]{:S(2)}, u32[]{:S(2)}) collective-permute-start(bf16[2,512,4,80]{1,3,2,0:T(8,128)(2,1)} %slice.48), channel_id=1, source_target_pairs={{4,0},{8,4},{12,8},{16,12},{20,16},{24,20},{28,24},{5,1},{9,5},{13... | collective-permute-start | bytes 1966088 | tf_op jit(solution)/shard_map/ppermute | solution.py:28
  27.0 0.9 broadcast_compare_fusion.4
  27.9 3.2 %collective-permute-start.3 = (bf16[2,512,4,80]{1,3,2,0:T(8,128)(2,1)}, bf16[2,512,4,80]{1,3,2,0:T(8,128)(2,1)}, u32[]{:S(2)}, u32[]{:S(2)}) collective-permute-start(bf16[2,512,4,80]{1,3,2,0:T(8,128)(2,1)} %slice.48), channel_id=1, source_target_pairs={{8,0},{12,4},{16,8},{20,12},{24,16},{28,20},{9,1},{13,5},{17,9},{2... | collective-permute-start | bytes 1966088 | tf_op jit(solution)/shard_map/ppermute | solution.py:28
  31.1 1.3 %collective-permute-start.2 = (bf16[2,512,4,80]{1,3,2,0:T(8,128)(2,1)}, bf16[2,512,4,80]{1,3,2,0:T(8,128)(2,1)}, u32[]{:S(2)}, u32[]{:S(2)}) collective-permute-start(bf16[2,512,4,80]{1,3,2,0:T(8,128)(2,1)} %slice.48), channel_id=1, source_target_pairs={{0,8},{4,12},{8,16},{12,20},{16,24},{20,28},{1,9},{5,13},{9,17},{1... | collective-permute-start | bytes 1966088 | tf_op jit(solution)/shard_map/ppermute | solution.py:28
  32.4 2.7 %collective-permute-start = (bf16[2,512,4,80]{1,3,2,0:T(8,128)(2,1)}, bf16[2,512,4,80]{1,3,2,0:T(8,128)(2,1)}, u32[]{:S(2)}, u32[]{:S(2)}) collective-permute-start(bf16[2,512,4,80]{1,3,2,0:T(8,128)(2,1)} %slice.48), channel_id=1, source_target_pairs={{0,4},{4,8},{8,12},{12,16},{16,20},{20,24},{24,28},{1,5},{5,9},{9,... | collective-permute-start | bytes 1966088 | tf_op jit(solution)/shard_map/ppermute | solution.py:28
  35.1 0.1 fusion.100
  35.2 0.3 copy.31
  35.5 0.1 squeeze.35
  35.6 0.3 copy.30
  35.9 0.1 squeeze.34
  36.0 0.3 copy.29
  36.3 0.1 squeeze.33
  36.4 1.0 %fusion = (f32[512,4]{0,1:T(4,128)S(1)}, f32[4,512,512]{2,1,0:T(8,128)S(1)}) fusion(pred[512,512]{0,1:T(8,128)(4,1)S(1)} %get-tuple-element.23, bf16[512,4,80]{0,2,1:T(8,128)(2,1)S(1)} %squeeze.33, bf16[512,4,80]{0,2,1:T(8,128)(2,1)S(1)} %squeeze.34), kind=kOutput, calls=%fused_computation.10 | convolution fusion | flops 170915840 | bytes 5120000 | tf_op jit(solution)/shard_map/qhd,khd->qhk/dot_general | solution.py:39
  37.4 5.1 %collective-permute-done.1 = bf16[2,512,4,80]{1,3,2,0:T(8,128)(2,1)} collective-permute-done((bf16[2,512,4,80]{1,3,2,0:T(8,128)(2,1)}, bf16[2,512,4,80]{1,3,2,0:T(8,128)(2,1)}, u32[]{:S(2)}, u32[]{:S(2)}) %collective-permute-start.1) | collective-permute-done | bytes 655392 | tf_op jit(solution)/shard_map/ppermute | solution.py:28
  42.5 1.9 %fusion.2 = (f32[512,4]{0,1:T(4,128)S(1)}, f32[4,512,512]{2,1,0:T(8,128)S(1)}) fusion(pred[512,512]{0,1:T(8,128)(4,1)S(1)} %get-tuple-element.24, bf16[512,4,80]{0,2,1:T(8,128)(2,1)S(1)} %squeeze.34, bf16[2,512,4,80]{1,3,2,0:T(8,128)(2,1)} %collective-permute-done.1), kind=kOutput, calls=%fused_computation.12 | convolution fusion | flops 170915840 | bytes 5120000 | tf_op jit(solution)/shard_map/qhd,khd->qhk/dot_general | solution.py:39
  44.4 4.5 %collective-permute-done.2 = bf16[2,512,4,80]{1,3,2,0:T(8,128)(2,1)} collective-permute-done((bf16[2,512,4,80]{1,3,2,0:T(8,128)(2,1)}, bf16[2,512,4,80]{1,3,2,0:T(8,128)(2,1)}, u32[]{:S(2)}, u32[]{:S(2)}) %collective-permute-start.2) | collective-permute-done | bytes 655392 | tf_op jit(solution)/shard_map/ppermute | solution.py:28
  48.9 1.9 %fusion.3 = (f32[512,4]{0,1:T(4,128)S(1)}, f32[4,512,512]{2,1,0:T(8,128)S(1)}) fusion(pred[512,512]{0,1:T(8,128)(4,1)S(1)} %get-tuple-element.25, bf16[512,4,80]{0,2,1:T(8,128)(2,1)S(1)} %squeeze.34, bf16[2,512,4,80]{1,3,2,0:T(8,128)(2,1)} %collective-permute-done.2), kind=kOutput, calls=%fused_computation.13 | convolution fusion | flops 170915840 | bytes 5120000 | tf_op jit(solution)/shard_map/qhd,khd->qhk/dot_general | solution.py:39
  50.9 4.2 %collective-permute-done.3 = bf16[2,512,4,80]{1,3,2,0:T(8,128)(2,1)} collective-permute-done((bf16[2,512,4,80]{1,3,2,0:T(8,128)(2,1)}, bf16[2,512,4,80]{1,3,2,0:T(8,128)(2,1)}, u32[]{:S(2)}, u32[]{:S(2)}) %collective-permute-start.3) | collective-permute-done | bytes 655392 | tf_op jit(solution)/shard_map/ppermute | solution.py:28
  55.1 1.9 %fusion.4 = (f32[512,4]{0,1:T(4,128)S(1)}, f32[4,512,512]{2,1,0:T(8,128)S(1)}) fusion(pred[512,512]{0,1:T(8,128)(4,1)S(1)} %get-tuple-element.26, bf16[512,4,80]{0,2,1:T(8,128)(2,1)S(1)} %squeeze.34, bf16[2,512,4,80]{1,3,2,0:T(8,128)(2,1)} %collective-permute-done.3), kind=kOutput, calls=%fused_computation.14 | convolution fusion | flops 170915840 | bytes 5120000 | tf_op jit(solution)/shard_map/qhd,khd->qhk/dot_general | solution.py:39
  57.0 6.0 %collective-permute-done = bf16[2,512,4,80]{1,3,2,0:T(8,128)(2,1)} collective-permute-done((bf16[2,512,4,80]{1,3,2,0:T(8,128)(2,1)}, bf16[2,512,4,80]{1,3,2,0:T(8,128)(2,1)}, u32[]{:S(2)}, u32[]{:S(2)}) %collective-permute-start) | collective-permute-done | bytes 655392 | tf_op jit(solution)/shard_map/ppermute | solution.py:28
  63.1 1.9 %fusion.1 = (f32[512,4]{0,1:T(4,128)S(1)}, f32[4,512,512]{2,1,0:T(8,128)S(1)}) fusion(pred[512,512]{0,1:T(8,128)(4,1)S(1)} %get-tuple-element.27, bf16[512,4,80]{0,2,1:T(8,128)(2,1)S(1)} %squeeze.34, bf16[2,512,4,80]{1,3,2,0:T(8,128)(2,1)} %collective-permute-done), kind=kOutput, calls=%fused_computation.11 | convolution fusion | flops 170915840 | bytes 5120000 | tf_op jit(solution)/shard_map/qhd,khd->qhk/dot_general | solution.py:39
  65.0 1.0 %fusion.13 = f32[512,4]{0,1:T(4,128)S(1)} fusion(f32[4,512,512]{2,1,0:T(8,128)S(1)} %get-tuple-element.34, f32[512,4]{0,1:T(4,128)S(1)} %get-tuple-element.10, pred[512,512]{0,1:T(8,128)(4,1)S(1)} %get-tuple-element.26), kind=kLoop, calls=%fused_computation.23 | loop fusion | flops 5240832 | bytes 4472832 | tf_op jit(solution)/shard_map/reduce_sum | solution.py:46
  66.1 1.1 %fusion.11 = f32[512,4]{0,1:T(4,128)S(1)} fusion(f32[4,512,512]{2,1,0:T(8,128)S(1)} %get-tuple-element.36, f32[512,4]{0,1:T(4,128)S(1)} %get-tuple-element.11, pred[512,512]{0,1:T(8,128)(4,1)S(1)} %get-tuple-element.25), kind=kLoop, calls=%fused_computation.21 | loop fusion | flops 5240832 | bytes 4472832 | tf_op jit(solution)/shard_map/reduce_sum | solution.py:46
  67.1 1.0 %fusion.9 = f32[512,4]{0,1:T(4,128)S(1)} fusion(f32[4,512,512]{2,1,0:T(8,128)S(1)} %get-tuple-element.38, f32[512,4]{0,1:T(4,128)S(1)} %get-tuple-element.12, pred[512,512]{0,1:T(8,128)(4,1)S(1)} %get-tuple-element.24), kind=kLoop, calls=%fused_computation.19 | loop fusion | flops 5240832 | bytes 4472832 | tf_op jit(solution)/shard_map/reduce_sum | solution.py:46
  68.2 1.1 %fusion.5 = f32[512,4]{0,1:T(4,128)S(1)} fusion(f32[4,512,512]{2,1,0:T(8,128)S(1)} %get-tuple-element.42, f32[512,4]{0,1:T(4,128)S(1)} %get-tuple-element.22, pred[512,512]{0,1:T(8,128)(4,1)S(1)} %get-tuple-element.23), kind=kLoop, calls=%fused_computation.15 | loop fusion | flops 5240832 | bytes 4472832 | tf_op jit(solution)/shard_map/reduce_sum | solution.py:46
  69.2 1.1 %fusion.7 = f32[512,4]{0,1:T(4,128)S(1)} fusion(f32[4,512,512]{2,1,0:T(8,128)S(1)} %get-tuple-element.40, f32[512,4]{0,1:T(4,128)S(1)} %get-tuple-element.13, pred[512,512]{0,1:T(8,128)(4,1)S(1)} %get-tuple-element.27), kind=kLoop, calls=%fused_computation.17 | loop fusion | flops 5240832 | bytes 4472832 | tf_op jit(solution)/shard_map/reduce_sum | solution.py:46
  70.3 1.5 %fusion.69 = f32[512,4,80]{0,2,1:T(8,128)S(1)} fusion(bf16[512,4,80]{0,2,1:T(8,128)(2,1)S(1)} %squeeze.35, f32[4,512,512]{2,1,0:T(8,128)S(1)} %get-tuple-element.42, f32[512,4]{0,1:T(4,128)S(1)} %get-tuple-element.22, pred[512,512]{0,1:T(8,128)(4,1)S(1)} %get-tuple-element.23, f32[512,4]{0,1:T(4,128)S(1)} %get-tuple-element.9, ...), kind=kOutput, calls=%fused_computation.48 | convolution fusion | flops 173342720 | bytes 5464064 | tf_op jit(solution)/shard_map/qhk,khd->qhd/dot_general | solution.py:47
  71.9 2.3 %fusion.42 = f32[512,4,80]{0,2,1:T(8,128)S(1)} fusion(f32[4,512,512]{2,1,0:T(8,128)S(1)} %get-tuple-element.34, f32[512,4]{0,1:T(4,128)S(1)} %get-tuple-element.10, pred[512,512]{0,1:T(8,128)(4,1)S(1)} %get-tuple-element.26, bf16[2,512,4,80]{1,3,2,0:T(8,128)(2,1)} %collective-permute-done.3), kind=kOutput, calls=%fused_computation.39 | convolution fusion | flops 173015040 | bytes 5447680 | tf_op jit(solution)/shard_map/qhk,khd->qhd/dot_general | solution.py:47
  74.2 2.3 %fusion.39 = f32[512,4,80]{0,2,1:T(8,128)S(1)} fusion(f32[4,512,512]{2,1,0:T(8,128)S(1)} %get-tuple-element.36, f32[512,4]{0,1:T(4,128)S(1)} %get-tuple-element.11, pred[512,512]{0,1:T(8,128)(4,1)S(1)} %get-tuple-element.25, bf16[2,512,4,80]{1,3,2,0:T(8,128)(2,1)} %collective-permute-done.2), kind=kOutput, calls=%fused_computation.38 | convolution fusion | flops 173015040 | bytes 5447680 | tf_op jit(solution)/shard_map/qhk,khd->qhd/dot_general | solution.py:47
  76.5 2.3 %fusion.36 = f32[512,4,80]{0,2,1:T(8,128)S(1)} fusion(f32[4,512,512]{2,1,0:T(8,128)S(1)} %get-tuple-element.38, f32[512,4]{0,1:T(4,128)S(1)} %get-tuple-element.12, pred[512,512]{0,1:T(8,128)(4,1)S(1)} %get-tuple-element.24, bf16[2,512,4,80]{1,3,2,0:T(8,128)(2,1)} %collective-permute-done.1), kind=kOutput, calls=%fused_computation.37 | convolution fusion | flops 173015040 | bytes 5447680 | tf_op jit(solution)/shard_map/qhk,khd->qhd/dot_general | solution.py:47
  78.8 2.4 %fusion.75 = bf16[512,4,80]{0,2,1:T(8,128)(2,1)S(1)} fusion(f32[512,4,80]{0,2,1:T(8,128)S(1)} %fusion.42, f32[512,4,80]{0,2,1:T(8,128)S(1)} %fusion.39, f32[512,4,80]{0,2,1:T(8,128)S(1)} %fusion.36, f32[512,4,80]{0,2,1:T(8,128)S(1)} %fusion.69, f32[4,512,512]{2,1,0:T(8,128)S(1)} %get-tuple-element.40, f32[512,4]{0,1:T(4,128)S(1)} %get-tuple-element.13, ...), kind=kOutput, calls=%fused_computation.50 | convolution fusion | flops 174489600 | bytes 7774208 | tf_op jit(solution)/shard_map/qhk,khd->qhd/dot_general | solution.py:47
  81.2 0.1 all_to_all.18
  81.4 9.1 %all_to_all.24 = bf16[4,128,320]{1,2,0:T(8,128)(2,1)S(1)} all-to-all(bf16[4,128,320]{1,2,0:T(8,128)(2,1)S(1)} %copy.38), channel_id=1, replica_groups=mesh['wide'=8,'grp'=4] {'grp'}, dimensions={0} | all-to-all | bytes 655360 | tf_op jit(solution)/shard_map/all_to_all | solution.py:117
  90.4 0.9 copy.39
  (4 shorter events, 0.1 us)
Async XLA Ops:
  2.4 6.0 %copy-start = (s32[32]{0:T(128)S(1)}, s32[32]{0:T(128)}, u32[]{:S(2)}) copy-start(s32[32]{0:T(128)} %param.7) | copy-start | bytes 388
  4.8 17.2 %all-to-all-start = ((bf16[4,3,128,320]{2,3,1,0:T(8,128)(2,1)}), bf16[4,3,128,320]{2,3,1,0:T(8,128)(2,1)S(1)}, u32[]{:S(2)}, u32[]{:S(2)}) async-start(bf16[4,3,128,320]{2,3,1,0:T(8,128)(2,1)} %pad_maximum_fusion.1), calls=%async_computation | async-start | bytes 1966080 | tf_op jit(solution)/shard_map/all_to_all | solution.py:15
  23.7 18.7 %collective-permute-start.1 = (bf16[2,512,4,80]{1,3,2,0:T(8,128)(2,1)}, bf16[2,512,4,80]{1,3,2,0:T(8,128)(2,1)}, u32[]{:S(2)}, u32[]{:S(2)}) collective-permute-start(bf16[2,512,4,80]{1,3,2,0:T(8,128)(2,1)} %slice.48), channel_id=1, source_target_pairs={{4,0},{8,4},{12,8},{16,12},{20,16},{24,20},{28,24},{5,1},{9,5},{13... | collective-permute-start | bytes 1966088 | tf_op jit(solution)/shard_map/ppermute | solution.py:28
  27.9 27.2 %collective-permute-start.3 = (bf16[2,512,4,80]{1,3,2,0:T(8,128)(2,1)}, bf16[2,512,4,80]{1,3,2,0:T(8,128)(2,1)}, u32[]{:S(2)}, u32[]{:S(2)}) collective-permute-start(bf16[2,512,4,80]{1,3,2,0:T(8,128)(2,1)} %slice.48), channel_id=1, source_target_pairs={{8,0},{12,4},{16,8},{20,12},{24,16},{28,20},{9,1},{13,5},{17,9},{2... | collective-permute-start | bytes 1966088 | tf_op jit(solution)/shard_map/ppermute | solution.py:28
  31.1 17.8 %collective-permute-start.2 = (bf16[2,512,4,80]{1,3,2,0:T(8,128)(2,1)}, bf16[2,512,4,80]{1,3,2,0:T(8,128)(2,1)}, u32[]{:S(2)}, u32[]{:S(2)}) collective-permute-start(bf16[2,512,4,80]{1,3,2,0:T(8,128)(2,1)} %slice.48), channel_id=1, source_target_pairs={{0,8},{4,12},{8,16},{12,20},{16,24},{20,28},{1,9},{5,13},{9,17},{1... | collective-permute-start | bytes 1966088 | tf_op jit(solution)/shard_map/ppermute | solution.py:28
  32.4 30.7 %collective-permute-start = (bf16[2,512,4,80]{1,3,2,0:T(8,128)(2,1)}, bf16[2,512,4,80]{1,3,2,0:T(8,128)(2,1)}, u32[]{:S(2)}, u32[]{:S(2)}) collective-permute-start(bf16[2,512,4,80]{1,3,2,0:T(8,128)(2,1)} %slice.48), channel_id=1, source_target_pairs={{0,4},{4,8},{8,12},{12,16},{16,20},{20,24},{24,28},{1,5},{5,9},{9,... | collective-permute-start | bytes 1966088 | tf_op jit(solution)/shard_map/ppermute | solution.py:28
